TPU v7x, 256 devices: a whole 4x4x8 slice. The times are simulated.
256 devices in a mesh: gx: 16 (over z_lo, x, core), gy: 4 (over y), tx: 4 (over z_hi).
Axes of the slice: x: 4, y: 4, z: 8 (z_hi: 4, z_lo: 2; z = z_hi * 2 + z_lo), core: 2. Of those that a mesh axis runs over, the one named last changes fastest.
Arguments:
- src_cell: int32 [8], P('tx'), may hold values from 0 to 524287
- basis: bfloat16 [16, 2, 3, 8, 128, 512], P('tx', None, None, None, 'gx', 'gy'), as said below
- images: bfloat16 [16, 2, 3, 8, 128, 512], P('tx', None, None, None, 'gx', 'gy'), as said below
- induction: bfloat16 [3, 8, 128, 512], P(None, 'tx', 'gx', 'gy'), may hold values from 0.25 to 4
Outputs:
- solution: float32 [8, 2, 3, 8, 128, 512], P('tx', None, None, None, 'gx', 'gy')
- residual: float32 [8, 2, 3, 8, 128, 512], P('tx', None, None, None, 'gx', 'gy')
Inputs may be any that keep to these rules, and one draw needn't show every extreme that they name: `basis`: entries of order one. `images`: entries of order one.
All inputs are finite; a program needn't handle non-finite values.
Results may differ from a plain program's by a relative error of at most 0.0003.
Values may be sent and summed in bfloat16 or wider, within the bound.
No kernel may reach another device: no remote copies, remote signals or barrier semaphores. Data moves between devices by JAX's collectives and lax.ppermute only.
A program may use at most 64 MiB of HBM per device.

v0:
```python
import jax
import jax.numpy as jnp
from jax import lax
from jax.sharding import PartitionSpec as P

CYCLES = 2
ARNOLDI = 2
eps = 1e-06


def with_halo(x, sides, width):
    for axis, dim in sides:
        size, length = (lax.axis_size(axis), x.shape[dim])
        up = [(i, (i + 1) % size) for i in range(size - 1)]
        down = [(j, i) for i, j in up]
        last = lax.slice_in_dim(x, length - width, length, axis=dim)
        initial = lax.slice_in_dim(x, 0, width, axis=dim)
        before = lax.ppermute(last, axis, up)
        after = lax.ppermute(initial, axis, down)
        x = jnp.concatenate([before, x, after], axis=dim)
    return x


def differ(field, axis, forward):
    axis = field.ndim + axis
    count = field.shape[axis]
    delta = lax.slice_in_dim(field, 1, count, axis=axis) - lax.slice_in_dim(
        field, 0, count - 1, axis=axis
    )
    zero = jnp.zeros_like(lax.slice_in_dim(field, 0, 1, axis=axis))
    if forward:
        return jnp.concatenate([delta, zero], axis=axis)
    return jnp.concatenate([zero, delta], axis=axis)


def curl_curl(padded):
    e_x = padded[..., 0, :, :, :]
    e_y = padded[..., 1, :, :, :]
    e_z = padded[..., 2, :, :, :]
    b_x = differ(e_z, -1, True) - differ(e_y, -3, True)
    b_y = differ(e_x, -3, True) - differ(e_z, -2, True)
    b_z = differ(e_y, -2, True) - differ(e_x, -1, True)
    c_x = differ(b_z, -1, False) - differ(b_y, -3, False)
    c_y = differ(b_x, -3, False) - differ(b_z, -2, False)
    c_z = differ(b_y, -2, False) - differ(b_x, -1, False)
    whole = jnp.stack([c_x, c_y, c_z], axis=-4)
    return whole[..., 1:-1, 1:-1, 1:-1]


def apply_operator(field, induct):
    framed = with_halo(field, (("gx", 4), ("gy", 5)), 1)
    padded = jnp.pad(framed, [(0, 0), (0, 0), (0, 0), (1, 1), (0, 0), (0, 0)])
    curled = curl_curl(padded)
    real_part = curled[:, 0] - induct[None] * field[:, 1]
    imag_part = curled[:, 1] + induct[None] * field[:, 0]
    return jnp.stack([real_part, imag_part], axis=1)


def source_field(cells, z_pos, x_pos, y_pos, size_x, size_y, induct):
    plane = size_x * size_y
    src_z = cells // plane
    rest = cells % plane
    src_x = rest // size_y
    src_y = rest % size_y
    d_z = (z_pos[None, :] - src_z[:, None]).astype(jnp.float32)
    d_x = (x_pos[None, :] - src_x[:, None]).astype(jnp.float32)
    d_y = (y_pos[None, :] - src_y[:, None]).astype(jnp.float32)
    dist = jnp.sqrt(
        d_z[:, :, None, None] ** 2 + d_x[:, None, :, None] ** 2 + d_y[:, None, None, :] ** 2
    )
    primary = jnp.exp(-dist / ((size_x + size_y) / 8.0))
    weights = jnp.array([1.0, 0.5, 0.25], dtype=jnp.float32)
    real_part = (induct - 1.0)[None] * weights[None, :, None, None, None] * primary[:, None]
    return jnp.stack([real_part, 0.5 * real_part], axis=1)


def inner_basis(vectors, field):
    return jnp.einsum(
        "kpczxy,spczxy->ks",
        vectors,
        field,
        precision=lax.Precision.HIGHEST,
        preferred_element_type=jnp.float32,
    )


def combine(coeffs, vectors):
    return jnp.einsum(
        "ks,kpczxy->spczxy",
        coeffs,
        vectors,
        precision=lax.Precision.HIGHEST,
        preferred_element_type=jnp.float32,
    )


def per_source(left, right):
    return jnp.sum(left * right, axis=(1, 2, 3, 4, 5))


def expand(values):
    return values[:, None, None, None, None, None]


def small_solve(matrix, rhs):
    factor = jnp.linalg.cholesky(matrix)
    return jax.scipy.linalg.cho_solve((factor, True), rhs)


def on_device(src_cell, basis, images, induction):
    all_basis, all_images, gathered = (
        lax.all_gather(basis, "tx", axis=0, tiled=True),
        lax.all_gather(images, "tx", axis=0, tiled=True),
        lax.all_gather(induction, "tx", axis=1, tiled=True),
    )
    induct = gathered.astype(jnp.float32)
    depth = basis.shape[3]
    width_x = basis.shape[4]
    width_y = basis.shape[5]
    size_x = width_x * lax.axis_size("gx")
    size_y = width_y * lax.axis_size("gy")
    z_pos = jnp.arange(depth, dtype=jnp.int32)
    x_pos = lax.axis_index("gx") * width_x + jnp.arange(width_x, dtype=jnp.int32)
    y_pos = lax.axis_index("gy") * width_y + jnp.arange(width_y, dtype=jnp.int32)
    rhs = source_field(src_cell, z_pos, x_pos, y_pos, size_x, size_y, induct)
    gram_part = jnp.einsum(
        "kpczxy,lpczxy->kl", all_images, all_images, preferred_element_type=jnp.float32
    )
    gram, start_inner = lax.psum((gram_part, inner_basis(all_images, rhs)), ("gx", "gy"))
    factor = jnp.linalg.cholesky(gram)
    h_zero = jax.scipy.linalg.cho_solve((factor, True), start_inner)
    residual = rhs - combine(h_zero, all_images)
    solution = combine(h_zero, all_basis)
    for cycle in range(CYCLES):
        beta = jnp.sqrt(lax.psum(per_source(residual, residual), ("gx", "gy")) + eps)
        krylov = [residual / expand(beta)]
        h_cols = []
        g_cols = []
        for step in range(ARNOLDI):
            work = apply_operator(krylov[step], induct)
            g_raw = lax.psum(inner_basis(all_images, work), ("gx", "gy"))
            g_now = jax.scipy.linalg.cho_solve((factor, True), g_raw)
            work = work - combine(g_now, all_images)
            h_now = lax.psum(jnp.stack([per_source(vec, work) for vec in krylov]), ("gx", "gy"))
            for index in range(step + 1):
                work = work - expand(h_now[index]) * krylov[index]
            h_next = jnp.sqrt(lax.psum(per_source(work, work), ("gx", "gy")) + eps)
            krylov.append(work / expand(h_next))
            pad_rows = jnp.zeros((ARNOLDI - step - 1, h_next.shape[0]), dtype=jnp.float32)
            h_cols.append(jnp.concatenate([h_now, h_next[None], pad_rows], axis=0))
            g_cols.append(g_now)
        hess = jnp.stack(h_cols, axis=1)
        g_all = jnp.stack(g_cols, axis=1)
        normal = jnp.einsum("ijs,iks->sjk", hess, hess, precision=lax.Precision.HIGHEST)
        target = beta[:, None] * jnp.transpose(hess[0])
        y_coef = jax.vmap(small_solve)(normal, target)
        update = expand(y_coef[:, 0]) * krylov[0]
        step = 1
        update = update + expand(y_coef[:, step]) * krylov[step]
        u_coef = jnp.einsum("kjs,sj->ks", g_all, y_coef, precision=lax.Precision.HIGHEST)
        solution = solution + update - combine(u_coef, all_basis)
        first = jnp.zeros((ARNOLDI + 1, beta.shape[0]), dtype=jnp.float32).at[0].set(beta)
        t_coef = first - jnp.einsum("ijs,sj->is", hess, y_coef, precision=lax.Precision.HIGHEST)
        residual = expand(t_coef[0]) * krylov[0]
        for index in range(1, ARNOLDI + 1):
            residual = residual + expand(t_coef[index]) * krylov[index]
    return (solution, residual)


def solution(mesh):
    in_specs = (
        P("tx"),
        P("tx", None, None, None, "gx", "gy"),
        P("tx", None, None, None, "gx", "gy"),
        P(None, "tx", "gx", "gy"),
    )
    out_specs = (P("tx", None, None, None, "gx", "gy"), P("tx", None, None, None, "gx", "gy"))
    return jax.shard_map(
        on_device, mesh=mesh, in_specs=in_specs, out_specs=out_specs, check_vma=False
    )
```

profile of v0, /device:TPU:40, one launch (start us, length us, event | category | flops | bytes accessed | tf_op | source)
XLA Modules:
  0.0 2366.0 jit_solution(5453150176349590648)
XLA Ops:
  7.9 16.6 all_gather.10
  26.5 26.6 %all-gather.3.cloned.1.call-done = bf16[16,2,3,8,8,128]{5,4,3,2,1,0:T(8,128)(2,1)} async-done(((bf16[4,2,3,8,8,128]{5,4,3,2,1,0:T(8,128)(2,1)}), bf16[16,2,3,8,8,128]{5,4,3,2,1,0:T(8,128)(2,1)}) %all-gather.3.cloned.1.call-update) | async-done | bytes 1572880 | tf_op jit(solution)/shard_map/all_gather | solution.py:113
  53.1 5.4 convolution_bitcast_fusion
  58.5 3.7 convolution_bitcast_fusion.8
  62.2 144.3 %all-reduce.54 = (f32[16,2]{0,1:T(2,128)S(1)}, f32[16,16]{0,1:T(8,128)S(1)}) all-reduce(f32[16,2]{0,1:T(2,128)S(1)} %convolution_bitcast_fusion.8, f32[16,16]{0,1:T(8,128)S(1)} %convolution_bitcast_fusion), channel_id=1, replica_groups=mesh['gx'=16,'gy'=4,'tx'=4] {'gx','gy'}, use_global_device_ids=true, to_apply=%region_3.4 | all-reduce | flops 288 | bytes 2304 | tf_op jit(solution)/shard_map/psum | solution.py:129
  214.2 143.8 %psum.114 = f32[2]{0:T(128)S(1)} all-reduce(f32[2]{0:T(128)S(1)} %get-tuple-element.119), channel_id=1, replica_groups=mesh['gx'=16,'gy'=4,'tx'=4] {'gx','gy'}, use_global_device_ids=true, to_apply=%region_5.7 | all-reduce | flops 2 | bytes 16 | tf_op jit(solution)/shard_map/psum | solution.py:135
  360.2 5.8 collective-permute-start.1
  370.4 4.1 collective-permute-start.3
  374.6 4.7 collective-permute-done.2
  394.9 140.9 %psum.115 = f32[16,2]{0,1:T(2,128)S(1)} all-reduce(f32[16,2]{0,1:T(2,128)S(1)} %convolution_bitcast_fusion.7), channel_id=1, replica_groups=mesh['gx'=16,'gy'=4,'tx'=4] {'gx','gy'}, use_global_device_ids=true, to_apply=%region_6.8 | all-reduce | flops 32 | bytes 256 | tf_op jit(solution)/shard_map/psum | solution.py:141
  539.4 139.6 %psum.116 = f32[1,2]{1,0:T(1,128)S(1)} all-reduce(f32[1,2]{1,0:T(1,128)S(1)} %bitcast.337), channel_id=1, replica_groups=mesh['gx'=16,'gy'=4,'tx'=4] {'gx','gy'}, use_global_device_ids=true, to_apply=%region_8.10 | all-reduce | flops 2 | bytes 16 | tf_op jit(solution)/shard_map/psum | solution.py:144
  679.7 139.5 %psum.117 = f32[2]{0:T(128)S(1)} all-reduce(f32[2]{0:T(128)S(1)} %get-tuple-element.49), channel_id=1, replica_groups=mesh['gx'=16,'gy'=4,'tx'=4] {'gx','gy'}, use_global_device_ids=true, to_apply=%region_10.12 | all-reduce | flops 2 | bytes 16 | tf_op jit(solution)/shard_map/psum | solution.py:147
  821.4 5.8 collective-permute-start.5
  831.6 3.9 collective-permute-start.7
  835.6 4.9 collective-permute-done.6
  856.1 141.1 %psum.118 = f32[16,2]{0,1:T(2,128)S(1)} all-reduce(f32[16,2]{0,1:T(2,128)S(1)} %convolution_bitcast_fusion.6), channel_id=1, replica_groups=mesh['gx'=16,'gy'=4,'tx'=4] {'gx','gy'}, use_global_device_ids=true, to_apply=%region_11.13 | all-reduce | flops 32 | bytes 256 | tf_op jit(solution)/shard_map/psum | solution.py:141
  1000.9 139.0 %psum.119 = f32[2,2]{1,0:T(2,128)S(1)} all-reduce(f32[2,2]{1,0:T(2,128)S(1)} %pad_maximum_fusion.26), channel_id=1, replica_groups=mesh['gx'=16,'gy'=4,'tx'=4] {'gx','gy'}, use_global_device_ids=true, to_apply=%region_14.16 | all-reduce | flops 4 | bytes 32 | tf_op jit(solution)/shard_map/psum | solution.py:144
  1140.6 140.2 %psum.120 = f32[2]{0:T(128)S(1)} all-reduce(f32[2]{0:T(128)S(1)} %get-tuple-element.47), channel_id=1, replica_groups=mesh['gx'=16,'gy'=4,'tx'=4] {'gx','gy'}, use_global_device_ids=true, to_apply=%region_16.18 | all-reduce | flops 2 | bytes 16 | tf_op jit(solution)/shard_map/psum | solution.py:147
  1283.8 139.0 %psum.121 = f32[2]{0:T(128)S(1)} all-reduce(f32[2]{0:T(128)S(1)} %get-tuple-element.45), channel_id=1, replica_groups=mesh['gx'=16,'gy'=4,'tx'=4] {'gx','gy'}, use_global_device_ids=true, to_apply=%region_20.24 | all-reduce | flops 2 | bytes 16 | tf_op jit(solution)/shard_map/psum | solution.py:135
  1425.0 5.8 collective-permute-start.9
  1430.8 3.7 convolution_add_fusion
  1437.3 4.1 collective-permute-start.11
  1441.5 5.5 collective-permute-done.10
  1462.7 140.7 %psum.122 = f32[16,2]{0,1:T(2,128)S(1)} all-reduce(f32[16,2]{0,1:T(2,128)S(1)} %convolution_bitcast_fusion.5), channel_id=1, replica_groups=mesh['gx'=16,'gy'=4,'tx'=4] {'gx','gy'}, use_global_device_ids=true, to_apply=%region_21.25 | all-reduce | flops 32 | bytes 256 | tf_op jit(solution)/shard_map/psum | solution.py:141
  1607.0 138.7 %psum.123 = f32[1,2]{1,0:T(1,128)S(1)} all-reduce(f32[1,2]{1,0:T(1,128)S(1)} %bitcast.338), channel_id=1, replica_groups=mesh['gx'=16,'gy'=4,'tx'=4] {'gx','gy'}, use_global_device_ids=true, to_apply=%region_23.27 | all-reduce | flops 2 | bytes 16 | tf_op jit(solution)/shard_map/psum | solution.py:144
  1746.3 140.5 %psum.124 = f32[2]{0:T(128)S(1)} all-reduce(f32[2]{0:T(128)S(1)} %get-tuple-element.43), channel_id=1, replica_groups=mesh['gx'=16,'gy'=4,'tx'=4] {'gx','gy'}, use_global_device_ids=true, to_apply=%region_25.29 | all-reduce | flops 2 | bytes 16 | tf_op jit(solution)/shard_map/psum | solution.py:147
  1889.0 5.8 collective-permute-start.13
  1899.2 3.9 collective-permute-start.15
  1903.2 4.9 collective-permute-done.14
  1923.7 140.9 %psum.125 = f32[16,2]{0,1:T(2,128)S(1)} all-reduce(f32[16,2]{0,1:T(2,128)S(1)} %convolution_bitcast_fusion.4), channel_id=1, replica_groups=mesh['gx'=16,'gy'=4,'tx'=4] {'gx','gy'}, use_global_device_ids=true, to_apply=%region_26.30 | all-reduce | flops 32 | bytes 256 | tf_op jit(solution)/shard_map/psum | solution.py:141
  2068.3 139.0 %psum.126 = f32[2,2]{1,0:T(2,128)S(1)} all-reduce(f32[2,2]{1,0:T(2,128)S(1)} %pad_maximum_fusion.27), channel_id=1, replica_groups=mesh['gx'=16,'gy'=4,'tx'=4] {'gx','gy'}, use_global_device_ids=true, to_apply=%region_29.33 | all-reduce | flops 4 | bytes 32 | tf_op jit(solution)/shard_map/psum | solution.py:144
  2208.7 140.2 %psum.127 = f32[2]{0:T(128)S(1)} all-reduce(f32[2]{0:T(128)S(1)} %get-tuple-element.41), channel_id=1, replica_groups=mesh['gx'=16,'gy'=4,'tx'=4] {'gx','gy'}, use_global_device_ids=true, to_apply=%region_31.35 | all-reduce | flops 2 | bytes 16 | tf_op jit(solution)/shard_map/psum | solution.py:147
  (241 shorter events, 127.9 us)
Async XLA Ops:
  7.2 46.0 %all-gather.3.cloned.1.call-start = ((), (), s32[]{:S(2)}) async-start(), calls=%async_computation | async-start | bytes 1966080 | tf_op jit(solution)/shard_map/all_gather | solution.py:113
  7.9 1422.9 %all-gather.5.cloned.1.call-start = ((), (), s32[]{:S(2)}) async-start(), calls=%async_computation.1 | async-start | bytes 1966080 | tf_op jit(solution)/shard_map/all_gather | solution.py:112
  53.1 5.4 copy-start.1
  358.2 7.7 collective-permute-start
  360.2 7.5 collective-permute-start.1
  368.5 10.8 collective-permute-start.2
  370.4 10.8 collective-permute-start.3
  389.8 1.4 copy-start.2
  819.5 7.8 collective-permute-start.4
  821.4 7.5 collective-permute-start.5
  829.7 10.8 collective-permute-start.6
  831.6 10.8 collective-permute-start.7
  851.0 1.4 copy-start.3
  1423.1 11.5 collective-permute-start.8
  1425.0 9.5 collective-permute-start.9
  1435.4 11.7 collective-permute-start.10
  1437.3 11.7 collective-permute-start.11
  1457.6 1.4 copy-start.4
  1887.0 7.8 collective-permute-start.12
  1889.0 7.5 collective-permute-start.13
  1897.3 10.8 collective-permute-start.14
  1899.2 10.8 collective-permute-start.15
  1918.6 1.4 copy-start.5
  2349.7 4.0 copy-start
Sparse Core Ops, SparseCore 0:
  9.8 43.2 all-gather.2
  366.1 35.2 all-gather.4
where the time goes:
time: 2380 us; the launch traced here: 2370 us
  blocking collectives  2120 us (89%)
  waiting for transfers between devices  59.9 us (3%)
  starting transfers between devices  54.6 us (2%)
  matrix products  50.6 us (2%)
  other arithmetic  50.3 us (2%)
    psum x4, blocking collectives, on_device(): g_raw = lax.psum(inner_basis(all_images, work), ('gx', 'gy'))  564 us
    psum x4, blocking collectives, on_device(): h_next = jnp.sqrt(lax.psum(per_source(work, work), ('gx', 'gy')) + eps)  560 us
    psum x4, blocking collectives, on_device(): lax.psum(jnp.stack([per_source(vec, work) for vec in krylov]), ('gx', 'gy'))  556 us
    psum x2, blocking collectives, on_device(): lax.psum(per_source(residual, residual), ('gx', 'gy')) + eps  283 us
    psum x1, blocking collectives, on_device(): lax.psum((gram_part, inner_basis(all_images, rhs)), ('gx', 'gy'))  144 us
  transfers between devices with their start and end apart: 18, of which 12 were waited for; matrix products, arithmetic and copies ran while one was open for 2% of the time, Pallas kernels for 0%

commit v1 on v0

--- a/solution.py
+++ b/solution.py
@@ -126,7 +126,8 @@
     gram_part = jnp.einsum(
         "kpczxy,lpczxy->kl", all_images, all_images, preferred_element_type=jnp.float32
     )
-    gram, start_inner = lax.psum((gram_part, inner_basis(all_images, rhs)), ("gx", "gy"))
+    pass_lane_all = lambda local_array: lax.psum(lax.psum(local_array, "gx"), "gy")
+    gram, start_inner = pass_lane_all((gram_part, inner_basis(all_images, rhs)))
     factor = jnp.linalg.cholesky(gram)
     h_zero = jax.scipy.linalg.cho_solve((factor, True), start_inner)
     residual = rhs - combine(h_zero, all_images)

time: 2380 us -> 2270 us (0.954)
  blocking collectives: 2120 us -> 2020 us
    psum x1 -> x2, blocking collectives: 144 us -> 41.3 us  [the longest x1 32.5 us: on_device(): lax.psum(local_array, 'gx')]
where the time goes in v1:
time: 2270 us; the launch traced here: 2260 us
  blocking collectives  2020 us (89%)
  waiting for transfers between devices  59.9 us (3%)
  starting transfers between devices  54.6 us (2%)
  matrix products  50.6 us (2%)
  other arithmetic  50.3 us (2%)
    psum x4, blocking collectives, on_device(): g_raw = lax.psum(inner_basis(all_images, work), ('gx', 'gy'))  564 us
    psum x4, blocking collectives, on_device(): h_next = jnp.sqrt(lax.psum(per_source(work, work), ('gx', 'gy')) + eps)  560 us
    psum x4, blocking collectives, on_device(): lax.psum(jnp.stack([per_source(vec, work) for vec in krylov]), ('gx', 'gy'))  556 us
    psum x2, blocking collectives, on_device(): lax.psum(per_source(residual, residual), ('gx', 'gy')) + eps  280 us
  transfers between devices with their start and end apart: 18, of which 12 were waited for; matrix products, arithmetic and copies ran while one was open for 2% of the time, Pallas kernels for 0%

profile of v1, /device:TPU:40, one launch (start us, length us, event | category | flops | bytes accessed | tf_op | source)
XLA Modules:
  0.0 2260.3 jit_solution(12238891105085259908)
XLA Ops:
  7.9 16.6 all_gather.10
  26.5 26.6 %all-gather.3.cloned.1.call-done = bf16[16,2,3,8,8,128]{5,4,3,2,1,0:T(8,128)(2,1)} async-done(((bf16[4,2,3,8,8,128]{5,4,3,2,1,0:T(8,128)(2,1)}), bf16[16,2,3,8,8,128]{5,4,3,2,1,0:T(8,128)(2,1)}) %all-gather.3.cloned.1.call-update) | async-done | bytes 1572880 | tf_op jit(solution)/shard_map/all_gather | solution.py:113
  53.1 5.4 convolution_bitcast_fusion
  62.2 32.5 %all-reduce.54 = (f32[16,2]{0,1:T(2,128)S(1)}, f32[16,16]{0,1:T(8,128)S(1)}) all-reduce(f32[16,2]{0,1:T(2,128)S(1)} %convolution_bitcast_fusion.8, f32[16,16]{0,1:T(8,128)S(1)} %convolution_bitcast_fusion), channel_id=1, replica_groups=mesh['gx'=16,'gy'=4,'tx'=4] {'gx'}, use_global_device_ids=true, to_apply=%region_4.5 | all-reduce | flops 288 | bytes 2304 | tf_op jit(solution)/shard_map/psum | solution.py:129
  94.7 8.8 all-reduce.55
  111.2 141.1 %psum.130 = f32[2]{0:T(128)S(1)} all-reduce(f32[2]{0:T(128)S(1)} %get-tuple-element.121), channel_id=1, replica_groups=mesh['gx'=16,'gy'=4,'tx'=4] {'gx','gy'}, use_global_device_ids=true, to_apply=%region_7.9 | all-reduce | flops 2 | bytes 16 | tf_op jit(solution)/shard_map/psum | solution.py:136
  254.4 5.8 collective-permute-start.1
  264.7 4.1 collective-permute-start.3
  268.8 4.7 collective-permute-done.2
  289.2 140.9 %psum.131 = f32[16,2]{0,1:T(2,128)S(1)} all-reduce(f32[16,2]{0,1:T(2,128)S(1)} %convolution_bitcast_fusion.7), channel_id=1, replica_groups=mesh['gx'=16,'gy'=4,'tx'=4] {'gx','gy'}, use_global_device_ids=true, to_apply=%region_8.10 | all-reduce | flops 32 | bytes 256 | tf_op jit(solution)/shard_map/psum | solution.py:142
  433.7 139.6 %psum.132 = f32[1,2]{1,0:T(1,128)S(1)} all-reduce(f32[1,2]{1,0:T(1,128)S(1)} %bitcast.337), channel_id=1, replica_groups=mesh['gx'=16,'gy'=4,'tx'=4] {'gx','gy'}, use_global_device_ids=true, to_apply=%region_10.12 | all-reduce | flops 2 | bytes 16 | tf_op jit(solution)/shard_map/psum | solution.py:145
  574.0 139.6 %psum.133 = f32[2]{0:T(128)S(1)} all-reduce(f32[2]{0:T(128)S(1)} %get-tuple-element.51), channel_id=1, replica_groups=mesh['gx'=16,'gy'=4,'tx'=4] {'gx','gy'}, use_global_device_ids=true, to_apply=%region_12.14 | all-reduce | flops 2 | bytes 16 | tf_op jit(solution)/shard_map/psum | solution.py:148
  715.7 5.8 collective-permute-start.5
  725.9 3.9 collective-permute-start.7
  729.9 4.9 collective-permute-done.6
  750.4 141.1 %psum.134 = f32[16,2]{0,1:T(2,128)S(1)} all-reduce(f32[16,2]{0,1:T(2,128)S(1)} %convolution_bitcast_fusion.6), channel_id=1, replica_groups=mesh['gx'=16,'gy'=4,'tx'=4] {'gx','gy'}, use_global_device_ids=true, to_apply=%region_13.15 | all-reduce | flops 32 | bytes 256 | tf_op jit(solution)/shard_map/psum | solution.py:142
  895.2 139.0 %psum.135 = f32[2,2]{1,0:T(2,128)S(1)} all-reduce(f32[2,2]{1,0:T(2,128)S(1)} %pad_maximum_fusion.26), channel_id=1, replica_groups=mesh['gx'=16,'gy'=4,'tx'=4] {'gx','gy'}, use_global_device_ids=true, to_apply=%region_16.18 | all-reduce | flops 4 | bytes 32 | tf_op jit(solution)/shard_map/psum | solution.py:145
  1034.9 140.2 %psum.136 = f32[2]{0:T(128)S(1)} all-reduce(f32[2]{0:T(128)S(1)} %get-tuple-element.49), channel_id=1, replica_groups=mesh['gx'=16,'gy'=4,'tx'=4] {'gx','gy'}, use_global_device_ids=true, to_apply=%region_18.20 | all-reduce | flops 2 | bytes 16 | tf_op jit(solution)/shard_map/psum | solution.py:148
  1178.1 139.0 %psum.137 = f32[2]{0:T(128)S(1)} all-reduce(f32[2]{0:T(128)S(1)} %get-tuple-element.47), channel_id=1, replica_groups=mesh['gx'=16,'gy'=4,'tx'=4] {'gx','gy'}, use_global_device_ids=true, to_apply=%region_22.26 | all-reduce | flops 2 | bytes 16 | tf_op jit(solution)/shard_map/psum | solution.py:136
  1319.3 5.8 collective-permute-start.9
  1325.1 3.7 convolution_add_fusion
  1331.6 4.1 collective-permute-start.11
  1335.8 5.5 collective-permute-done.10
  1357.0 140.7 %psum.138 = f32[16,2]{0,1:T(2,128)S(1)} all-reduce(f32[16,2]{0,1:T(2,128)S(1)} %convolution_bitcast_fusion.5), channel_id=1, replica_groups=mesh['gx'=16,'gy'=4,'tx'=4] {'gx','gy'}, use_global_device_ids=true, to_apply=%region_23.27 | all-reduce | flops 32 | bytes 256 | tf_op jit(solution)/shard_map/psum | solution.py:142
  1501.3 138.7 %psum.139 = f32[1,2]{1,0:T(1,128)S(1)} all-reduce(f32[1,2]{1,0:T(1,128)S(1)} %bitcast.338), channel_id=1, replica_groups=mesh['gx'=16,'gy'=4,'tx'=4] {'gx','gy'}, use_global_device_ids=true, to_apply=%region_25.29 | all-reduce | flops 2 | bytes 16 | tf_op jit(solution)/shard_map/psum | solution.py:145
  1640.6 140.5 %psum.140 = f32[2]{0:T(128)S(1)} all-reduce(f32[2]{0:T(128)S(1)} %get-tuple-element.45), channel_id=1, replica_groups=mesh['gx'=16,'gy'=4,'tx'=4] {'gx','gy'}, use_global_device_ids=true, to_apply=%region_27.31 | all-reduce | flops 2 | bytes 16 | tf_op jit(solution)/shard_map/psum | solution.py:148
  1783.3 5.8 collective-permute-start.13
  1793.5 3.9 collective-permute-start.15
  1797.5 4.9 collective-permute-done.14
  1818.0 140.9 %psum.141 = f32[16,2]{0,1:T(2,128)S(1)} all-reduce(f32[16,2]{0,1:T(2,128)S(1)} %convolution_bitcast_fusion.4), channel_id=1, replica_groups=mesh['gx'=16,'gy'=4,'tx'=4] {'gx','gy'}, use_global_device_ids=true, to_apply=%region_28.32 | all-reduce | flops 32 | bytes 256 | tf_op jit(solution)/shard_map/psum | solution.py:142
  1962.6 139.0 %psum.142 = f32[2,2]{1,0:T(2,128)S(1)} all-reduce(f32[2,2]{1,0:T(2,128)S(1)} %pad_maximum_fusion.27), channel_id=1, replica_groups=mesh['gx'=16,'gy'=4,'tx'=4] {'gx','gy'}, use_global_device_ids=true, to_apply=%region_31.35 | all-reduce | flops 4 | bytes 32 | tf_op jit(solution)/shard_map/psum | solution.py:145
  2103.0 140.2 %psum.143 = f32[2]{0:T(128)S(1)} all-reduce(f32[2]{0:T(128)S(1)} %get-tuple-element.43), channel_id=1, replica_groups=mesh['gx'=16,'gy'=4,'tx'=4] {'gx','gy'}, use_global_device_ids=true, to_apply=%region_33.37 | all-reduce | flops 2 | bytes 16 | tf_op jit(solution)/shard_map/psum | solution.py:148
  (242 shorter events, 131.6 us)
Async XLA Ops:
  7.2 46.0 %all-gather.3.cloned.1.call-start = ((), (), s32[]{:S(2)}) async-start(), calls=%async_computation | async-start | bytes 1966080 | tf_op jit(solution)/shard_map/all_gather | solution.py:113
  7.9 1317.2 %all-gather.5.cloned.1.call-start = ((), (), s32[]{:S(2)}) async-start(), calls=%async_computation.1 | async-start | bytes 1966080 | tf_op jit(solution)/shard_map/all_gather | solution.py:112
  53.1 5.4 copy-start.1
  252.5 7.7 collective-permute-start
  254.4 7.5 collective-permute-start.1
  262.8 10.8 collective-permute-start.2
  264.7 10.8 collective-permute-start.3
  284.1 1.4 copy-start.2
  713.8 7.8 collective-permute-start.4
  715.7 7.5 collective-permute-start.5
  724.0 10.8 collective-permute-start.6
  725.9 10.8 collective-permute-start.7
  745.3 1.4 copy-start.3
  1317.4 11.5 collective-permute-start.8
  1319.3 9.5 collective-permute-start.9
  1329.7 11.7 collective-permute-start.10
  1331.6 11.7 collective-permute-start.11
  1351.9 1.4 copy-start.4
  1781.3 7.8 collective-permute-start.12
  1783.3 7.5 collective-permute-start.13
  1791.6 10.8 collective-permute-start.14
  1793.5 10.8 collective-permute-start.15
  1812.9 1.4 copy-start.5
  2244.0 4.0 copy-start
Sparse Core Ops, SparseCore 0:
  9.8 43.2 all-gather.2
  260.4 35.2 all-gather.4
